TPU v7x, 512 devices: a whole 4x8x8 slice. The times are simulated.
512 devices in a mesh: tok: 32 (over y, x), exp: 16 (over z, core).
Axes of the slice: x: 4, y: 8, z: 8, core: 2. Of those that a mesh axis runs over, the one named last changes fastest.
Arguments:
- tokens: bfloat16 [512, 6144], P('tok', 'exp'), may hold values from -6 to 6
- route_ids: int32 [512, 2], P('tok'), may hold values from 0 to 3, all different within a row; in each aligned block of 16 rows (0 to 15, 16 to 31, ...) at most 12 rows name the same one
- gate_codes: int32 [512, 2], P('tok'), may hold values from 1 to 255
- merge_labels: int32 [4], replicated, may hold values from 0 to 1, as said below
- freq_counts: int32 [4], replicated, may hold values from 1024 to 4096
- w_gate: bfloat16 [32768, 6144], P(('tok', 'exp')), may hold values from -0.078125 to 0.078125
- w_up: bfloat16 [32768, 6144], P(('tok', 'exp')), may hold values from -0.078125 to 0.078125
- w_down: bfloat16 [32768, 6144], P('tok', 'exp'), may hold values from -0.0625 to 0.0625
Outputs:
- initial_out: bfloat16 [512, 6144], P('tok', 'exp')
- merged_out: bfloat16 [512, 6144], P('tok', 'exp')
Inputs may be any that keep to these rules, and one draw needn't show every extreme that they name: `route_ids`: the 2 ids of a row differ. Among the 16 rows of one token shard no expert is named more than 12 times, a bound that some block reaches. `merge_labels`: experts with equal labels form one merge group; every group has exactly two experts.
All inputs are finite; a program needn't handle non-finite values.
Results may differ from a plain program's by a relative error of at most 0.0085.
Values may be sent and summed in bfloat16 or wider, within the bound.
A program may use at most 64 MiB of HBM per device.

v0:
```python
import jax
import jax.numpy as jnp
from jax import lax
from jax.sharding import PartitionSpec as P

EXPERTS = 4
TOP = 2
CAP = 12


def passed_along(value, axis, by):
    devices = lax.axis_size(axis)
    return lax.ppermute(value, axis, [(i, (i + by) % devices) for i in range(devices)])


def local(tokens, route_ids, gate_codes, merge_labels, freq_counts, w_gate, w_up, w_down):
    n_tok = lax.axis_size("tok")
    span = n_tok // EXPERTS
    expert = lax.axis_index("tok") // span
    tok_dev = tokens.shape[0]
    width = tokens.shape[1]
    flat = route_ids.reshape(-1)
    labels_idx = jnp.arange(EXPERTS, dtype=jnp.int32)
    picked = (flat[:, None] == labels_idx[None, :]).astype(jnp.int32)
    before = jnp.cumsum(picked, axis=0) - picked
    slot = jnp.sum(before * picked, axis=1)
    places = jnp.arange(CAP, dtype=jnp.int32)
    landing = picked.T[:, None, :] * (slot[None, None, :] == places[None, :, None]).astype(
        jnp.int32
    )
    landing = landing.reshape(EXPERTS, CAP, tok_dev, TOP)
    scale = gate_codes.astype(jnp.float32) / 256.0
    place_map = jnp.sum(landing, axis=3).astype(jnp.bfloat16)
    weighted = jnp.sum(landing.astype(jnp.float32) * scale[None, None, :, :], axis=3)
    packed = jnp.einsum(
        "ecn,nd->ecd", place_map, tokens, preferred_element_type=jnp.float32
    ).astype(jnp.bfloat16)
    copies = jnp.repeat(packed, span, axis=0)
    arrived = lax.all_to_all(copies, "tok", split_axis=0, concat_axis=0, tiled=True)
    rows_part = arrived.reshape(n_tok * CAP, width)
    rows = lax.all_gather(rows_part, "exp", axis=1, tiled=True)

    def project(gate_w, up_w, down_w):
        gate = jnp.einsum("sd,fd->sf", rows, gate_w, preferred_element_type=jnp.float32)
        upper = jnp.einsum("sd,fd->sf", rows, up_w, preferred_element_type=jnp.float32)
        hidden = (jax.nn.silu(gate) * upper).astype(jnp.bfloat16)
        units = lax.all_gather(hidden, "exp", axis=1, tiled=True)
        return jnp.dot(units, down_w, preferred_element_type=jnp.float32)

    first = project(w_gate, w_up, w_down)
    freq = freq_counts.astype(jnp.float32)
    own_label = jnp.sum(jnp.where(labels_idx == expert, merge_labels, 0))
    member = jnp.where(merge_labels == own_label, freq, jnp.float32(0.0))
    coef = member / jnp.sum(member)

    def weight_of(source):
        return jnp.sum(jnp.where(labels_idx == source, coef, jnp.float32(0.0)))

    own_weight = weight_of(expert)
    accums = (
        own_weight * w_gate.astype(jnp.float32),
        own_weight * w_up.astype(jnp.float32),
        own_weight * w_down.astype(jnp.float32),
    )
    for offset in range(1, EXPERTS):
        peers = passed_along((w_gate, w_up, w_down), "tok", offset * span)
        factor = weight_of((expert - offset) % EXPERTS)
        accums = (
            accums[0] + factor * peers[0].astype(jnp.float32),
            accums[1] + factor * peers[1].astype(jnp.float32),
            accums[2] + factor * peers[2].astype(jnp.float32),
        )
    second = project(
        accums[0].astype(jnp.bfloat16),
        accums[1].astype(jnp.bfloat16),
        accums[2].astype(jnp.bfloat16),
    )
    stacked = jnp.stack(
        [first.reshape(n_tok, CAP, width), second.reshape(n_tok, CAP, width)], axis=0
    )
    backs = lax.all_to_all(
        stacked.astype(jnp.bfloat16), "tok", split_axis=1, concat_axis=1, tiled=True
    ).astype(stacked.dtype)
    totals = jnp.sum(backs.reshape(2, EXPERTS, span, CAP, width), axis=2)
    final = jnp.einsum(
        "ecn,xecd->xnd",
        weighted,
        totals,
        precision=lax.Precision.HIGHEST,
        preferred_element_type=jnp.float32,
    )
    return (final[0].astype(jnp.bfloat16), final[1].astype(jnp.bfloat16))


def solution(mesh):
    return jax.shard_map(
        local,
        mesh=mesh,
        in_specs=(
            P("tok", "exp"),
            P("tok", None),
            P("tok", None),
            P(),
            P(),
            P(("tok", "exp"), None),
            P(("tok", "exp"), None),
            P("tok", "exp"),
        ),
        out_specs=(P("tok", "exp"), P("tok", "exp")),
        check_vma=False,
    )
```

profile of v0, /device:TPU:8, one launch (start us, length us, event | category | flops | bytes accessed | tf_op | source)
XLA Modules:
  0.0 296.3 jit_solution(11261646485899905770)
XLA Ops:
  9.6 24.7 %all_to_all.10 = bf16[32,12,384]{2,1,0:T(8,128)(2,1)S(1)} all-to-all(bf16[32,12,384]{2,1,0:T(8,128)(2,1)S(1)} %bitcast.34), channel_id=1, replica_groups=mesh['tok'=32,'exp'=16] {'tok'}, dimensions={0} | all-to-all | bytes 589824 | tf_op jit(solution)/shard_map/all_to_all | solution.py:39
  35.1 2.9 collective-permute-start
  38.0 5.1 %collective-permute-start.2 = (bf16[64,6144]{1,0:T(8,128)(2,1)S(1)}, bf16[64,6144]{1,0:T(8,128)(2,1)}, u32[]{:S(2)}, u32[]{:S(2)}) collective-permute-start(bf16[64,6144]{1,0:T(8,128)(2,1)S(1)} %copy-done.2), channel_id=1, source_target_pairs={{0,384},{16,400},{32,416},{48,432},{64,448},{80,464},{96,480},{112... | collective-permute-start | bytes 2359304 | tf_op jit(solution)/shard_map/ppermute | solution.py:13
  43.1 3.3 %collective-permute-start.1 = (bf16[64,6144]{1,0:T(8,128)(2,1)S(1)}, bf16[64,6144]{1,0:T(8,128)(2,1)}, u32[]{:S(2)}, u32[]{:S(2)}) collective-permute-start(bf16[64,6144]{1,0:T(8,128)(2,1)S(1)} %copy-done.2), channel_id=1, source_target_pairs={{0,256},{16,272},{32,288},{48,304},{64,320},{80,336},{96,352},{112... | collective-permute-start | bytes 2359304 | tf_op jit(solution)/shard_map/ppermute | solution.py:13
  46.5 2.9 collective-permute-start.3
  49.3 5.1 %collective-permute-start.5 = (bf16[64,6144]{1,0:T(8,128)(2,1)S(1)}, bf16[64,6144]{1,0:T(8,128)(2,1)}, u32[]{:S(2)}, u32[]{:S(2)}) collective-permute-start(bf16[64,6144]{1,0:T(8,128)(2,1)S(1)} %copy-done.3), channel_id=1, source_target_pairs={{0,384},{16,400},{32,416},{48,432},{64,448},{80,464},{96,480},{112... | collective-permute-start | bytes 2359304 | tf_op jit(solution)/shard_map/ppermute | solution.py:13
  56.4 2.0 fusion.25
  58.4 22.8 %all-gather.2.cloned.1.call-done = bf16[384,6144]{1,0:T(8,128)(2,1)} async-done(((bf16[384,384]{1,0:T(8,128)(2,1)}), bf16[384,6144]{1,0:T(8,128)(2,1)}) %all-gather.2.cloned.1.call-update) | async-done | bytes 4718608 | tf_op jit(solution)/shard_map/all_gather | solution.py:41
  81.2 4.0 %fusion.30 = f32[384,64]{0,1:T(8,128)S(1)} fusion(bf16[384,6144]{1,0:T(8,128)(2,1)} %all-gather.2.cloned.1.call-done, bf16[64,6144]{1,0:T(8,128)(2,1)S(1)} %copy-done.2), kind=kOutput, calls=%fused_computation.57 | convolution fusion | flops 301989888 | bytes 5603328 | tf_op jit(solution)/shard_map/sd,fd->sf/dot_general | solution.py:44
  85.3 1.6 fusion
  86.9 18.0 %all_gather.10 = bf16[384,1024]{0,1:T(8,128)(2,1)S(1)} all-gather(bf16[384,64]{0,1:T(8,128)(2,1)S(1)} %fusion), channel_id=1, replica_groups=mesh['tok'=32,'exp'=16] {'exp'}, dimensions={1}, use_global_device_ids=true | all-gather | bytes 835584 | tf_op jit(solution)/shard_map/all_gather | solution.py:47
  104.9 6.5 %collective-permute-start.4 = (bf16[64,6144]{1,0:T(8,128)(2,1)S(1)}, bf16[64,6144]{1,0:T(8,128)(2,1)}, u32[]{:S(2)}, u32[]{:S(2)}) collective-permute-start(bf16[64,6144]{1,0:T(8,128)(2,1)S(1)} %copy-done.3), channel_id=1, source_target_pairs={{0,256},{16,272},{32,288},{48,304},{64,320},{80,336},{96,352},{112... | collective-permute-start | bytes 2359304 | tf_op jit(solution)/shard_map/ppermute | solution.py:13
  112.1 2.6 collective-permute-start.6
  114.7 5.5 %collective-permute-start.8 = (bf16[1024,384]{1,0:T(8,128)(2,1)}, bf16[1024,384]{1,0:T(8,128)(2,1)S(1)}, u32[]{:S(2)}, u32[]{:S(2)}) collective-permute-start(bf16[1024,384]{1,0:T(8,128)(2,1)} %param.15), channel_id=1, source_target_pairs={{0,384},{16,400},{32,416},{48,432},{64,448},{80,464},{96,480},{112... | collective-permute-start | bytes 2359304 | tf_op jit(solution)/shard_map/ppermute | solution.py:13
  120.2 7.7 %fusion.3 = f32[384,64]{0,1:T(8,128)S(1)} fusion(bf16[384,6144]{1,0:T(8,128)(2,1)} %all-gather.2.cloned.1.call-done, bf16[64,6144]{1,0:T(8,128)(2,1)} %collective-permute-done.2, bf16[64,6144]{1,0:T(8,128)(2,1)} %collective-permute-done.1, bf16[64,6144]{1,0:T(8,128)(2,1)} %collective-permute-done, bf16[64,6144]{1,0:T(8,128)(2,1)S(1)} %copy-done.2, ...), kind=kOutput, calls=%fused_computation.12 | convolution fusion | flops 306708480 | bytes 7962640 | tf_op jit(solution)/shard_map/sd,fd->sf/dot_general | solution.py:44
  127.9 88.3 %collective-permute-done.3 = bf16[64,6144]{1,0:T(8,128)(2,1)} collective-permute-done((bf16[64,6144]{1,0:T(8,128)(2,1)S(1)}, bf16[64,6144]{1,0:T(8,128)(2,1)}, u32[]{:S(2)}, u32[]{:S(2)}) %collective-permute-start.3) | collective-permute-done | bytes 786464 | tf_op jit(solution)/shard_map/ppermute | solution.py:13
  216.3 1.9 collective-permute-start.7
  218.2 5.9 %multiply_convert_fusion = bf16[384,64]{0,1:T(8,128)(2,1)S(1)} fusion(f32[384,64]{0,1:T(8,128)S(1)} %fusion.3, bf16[384,6144]{1,0:T(8,128)(2,1)S(1)} %bitcast.33, bf16[64,6144]{1,0:T(8,128)(2,1)} %collective-permute-done.5, bf16[64,6144]{1,0:T(8,128)(2,1)} %collective-permute-done.4, bf16[64,6144]{1,0:T(8,128)(2,1)} %collective-permute-done.3, ...), kind=kOutput, calls=%fused_computation.27 | convolution fusion | flops 306855936 | bytes 8011792 | tf_op jit(solution)/shard_map/sd,fd->sf/dot_general | solution.py:45
  224.1 16.8 %all_gather.11 = bf16[384,1024]{0,1:T(8,128)(2,1)S(1)} all-gather(bf16[384,64]{0,1:T(8,128)(2,1)S(1)} %multiply_convert_fusion), channel_id=1, replica_groups=mesh['tok'=32,'exp'=16] {'exp'}, dimensions={1}, use_global_device_ids=true | all-gather | bytes 835584 | tf_op jit(solution)/shard_map/all_gather | solution.py:47
  241.0 4.5 %collective-permute-done.7 = bf16[1024,384]{1,0:T(8,128)(2,1)S(1)} collective-permute-done((bf16[1024,384]{1,0:T(8,128)(2,1)S(1)}, bf16[1024,384]{1,0:T(8,128)(2,1)S(1)}, u32[]{:S(2)}, u32[]{:S(2)}) %collective-permute-start.7) | collective-permute-done | bytes 786464 | tf_op jit(solution)/shard_map/ppermute | solution.py:13
  245.4 3.5 %convolution_convert_fusion = bf16[384,384]{1,0:T(8,128)(2,1)S(1)} fusion(bf16[384,1024]{0,1:T(8,128)(2,1)S(1)} %all_gather.11, bf16[1024,384]{1,0:T(8,128)(2,1)S(1)} %collective-permute-done.8, bf16[1024,384]{1,0:T(8,128)(2,1)S(1)} %collective-permute-done.7, bf16[1024,384]{1,0:T(8,128)(2,1)S(1)} %collective-permute-done.6, ...), kind=kOutput, calls=%fused_computation.3 | convolution fusion | flops 306855936 | bytes 4227088 | tf_op jit(solution)/shard_map/dot_general | solution.py:48
  249.2 1.4 copy.28
  250.6 20.4 %all-to-all-start.1 = ((bf16[2,32,12,384]{3,0,2,1:T(2,128)(2,1)}), bf16[2,32,12,384]{3,0,2,1:T(2,128)(2,1)S(1)}, u32[]{:S(2)}, u32[]{:S(2)}) async-start(bf16[2,32,12,384]{3,0,2,1:T(2,128)(2,1)} %copy.28), calls=%async_computation.1 | async-start | bytes 1179648 | tf_op jit(solution)/shard_map/all_to_all | solution.py:81
  271.2 16.8 %all-to-all-done.1 = bf16[2,32,12,384]{3,0,2,1:T(2,128)(2,1)S(1)} async-done(((bf16[2,32,12,384]{3,0,2,1:T(2,128)(2,1)}), bf16[2,32,12,384]{3,0,2,1:T(2,128)(2,1)S(1)}, u32[]{:S(2)}, u32[]{:S(2)}) %all-to-all-start.1) | async-done | bytes 589856 | tf_op jit(solution)/shard_map/all_to_all | solution.py:81
  (58 shorter events, 7.5 us)
Async XLA Ops:
  7.2 2.3 copy-start
  7.2 28.0 %copy-start.2 = (bf16[64,6144]{1,0:T(8,128)(2,1)S(1)}, bf16[64,6144]{1,0:T(8,128)(2,1)}, u32[]{:S(2)}) copy-start(bf16[64,6144]{1,0:T(8,128)(2,1)} %param.13) | copy-start | bytes 2359300
  7.2 39.3 %copy-start.3 = (bf16[64,6144]{1,0:T(8,128)(2,1)S(1)}, bf16[64,6144]{1,0:T(8,128)(2,1)}, u32[]{:S(2)}) copy-start(bf16[64,6144]{1,0:T(8,128)(2,1)} %param.14) | copy-start | bytes 2359300
  7.2 47.3 %copy-start.5 = (s32[4]{0:T(128)S(1)}, s32[4]{0:T(128)}, u32[]{:S(2)}) copy-start(s32[4]{0:T(128)} %param.11) | copy-start | bytes 52
  7.2 47.9 %copy-start.4 = (s32[4]{0:T(128)S(1)}, s32[4]{0:T(128)}, u32[]{:S(2)}) copy-start(s32[4]{0:T(128)} %param.12) | copy-start | bytes 52
  7.2 74.0 %all-gather.2.cloned.1.call-start = ((), (), s32[]{:S(2)}) async-start(), calls=%async_computation.2 | async-start | bytes 5013504 | tf_op jit(solution)/shard_map/all_gather | solution.py:41
  35.1 69.7 %collective-permute-start = (bf16[64,6144]{1,0:T(8,128)(2,1)S(1)}, bf16[64,6144]{1,0:T(8,128)(2,1)}, u32[]{:S(2)}, u32[]{:S(2)}) collective-permute-start(bf16[64,6144]{1,0:T(8,128)(2,1)S(1)} %copy-done.2), channel_id=1, source_target_pairs={{0,128},{16,144},{32,160},{48,176},{64,192},{80,208},{96,224},{112... | collective-permute-start | bytes 2359304 | tf_op jit(solution)/shard_map/ppermute | solution.py:13
  38.0 74.0 %collective-permute-start.2 = (bf16[64,6144]{1,0:T(8,128)(2,1)S(1)}, bf16[64,6144]{1,0:T(8,128)(2,1)}, u32[]{:S(2)}, u32[]{:S(2)}) collective-permute-start(bf16[64,6144]{1,0:T(8,128)(2,1)S(1)} %copy-done.2), channel_id=1, source_target_pairs={{0,384},{16,400},{32,416},{48,432},{64,448},{80,464},{96,480},{112... | collective-permute-start | bytes 2359304 | tf_op jit(solution)/shard_map/ppermute | solution.py:13
  43.1 71.6 %collective-permute-start.1 = (bf16[64,6144]{1,0:T(8,128)(2,1)S(1)}, bf16[64,6144]{1,0:T(8,128)(2,1)}, u32[]{:S(2)}, u32[]{:S(2)}) collective-permute-start(bf16[64,6144]{1,0:T(8,128)(2,1)S(1)} %copy-done.2), channel_id=1, source_target_pairs={{0,256},{16,272},{32,288},{48,304},{64,320},{80,336},{96,352},{112... | collective-permute-start | bytes 2359304 | tf_op jit(solution)/shard_map/ppermute | solution.py:13
  46.5 169.8 %collective-permute-start.3 = (bf16[64,6144]{1,0:T(8,128)(2,1)S(1)}, bf16[64,6144]{1,0:T(8,128)(2,1)}, u32[]{:S(2)}, u32[]{:S(2)}) collective-permute-start(bf16[64,6144]{1,0:T(8,128)(2,1)S(1)} %copy-done.3), channel_id=1, source_target_pairs={{0,128},{16,144},{32,160},{48,176},{64,192},{80,208},{96,224},{112... | collective-permute-start | bytes 2359304 | tf_op jit(solution)/shard_map/ppermute | solution.py:13
  49.3 168.9 %collective-permute-start.5 = (bf16[64,6144]{1,0:T(8,128)(2,1)S(1)}, bf16[64,6144]{1,0:T(8,128)(2,1)}, u32[]{:S(2)}, u32[]{:S(2)}) collective-permute-start(bf16[64,6144]{1,0:T(8,128)(2,1)S(1)} %copy-done.3), channel_id=1, source_target_pairs={{0,384},{16,400},{32,416},{48,432},{64,448},{80,464},{96,480},{112... | collective-permute-start | bytes 2359304 | tf_op jit(solution)/shard_map/ppermute | solution.py:13
  81.2 4.1 %copy-start.1 = (bf16[384,6144]{1,0:T(8,128)(2,1)S(1)}, bf16[384,6144]{1,0:T(8,128)(2,1)}, u32[]{:S(2)}) copy-start(bf16[384,6144]{1,0:T(8,128)(2,1)} %all-gather.2.cloned.1.call-done) | copy-start | bytes 14155780
  85.3 26.1 %copy-start.7 = (bf16[1024,384]{1,0:T(8,128)(2,1)S(1)}, bf16[1024,384]{1,0:T(8,128)(2,1)}, u32[]{:S(2)}) copy-start(bf16[1024,384]{1,0:T(8,128)(2,1)} %param.15) | copy-start | bytes 2359300
  104.9 113.3 %collective-permute-start.4 = (bf16[64,6144]{1,0:T(8,128)(2,1)S(1)}, bf16[64,6144]{1,0:T(8,128)(2,1)}, u32[]{:S(2)}, u32[]{:S(2)}) collective-permute-start(bf16[64,6144]{1,0:T(8,128)(2,1)S(1)} %copy-done.3), channel_id=1, source_target_pairs={{0,256},{16,272},{32,288},{48,304},{64,320},{80,336},{96,352},{112... | collective-permute-start | bytes 2359304 | tf_op jit(solution)/shard_map/ppermute | solution.py:13
  112.0 106.2 %slice-start = ((s8[4718592]{0:T(1024)(128)(4,1)}), s8[524288]{0:T(1024)(128)(4,1)S(1)}, s32[]{:S(2)}) async-start(s8[4718592]{0:T(1024)(128)(4,1)} %bitcast.32), calls=%async_computation.3 | async-start | bytes 1048576
  112.1 128.9 %collective-permute-start.6 = (bf16[1024,384]{1,0:T(8,128)(2,1)}, bf16[1024,384]{1,0:T(8,128)(2,1)S(1)}, u32[]{:S(2)}, u32[]{:S(2)}) collective-permute-start(bf16[1024,384]{1,0:T(8,128)(2,1)} %param.15), channel_id=1, source_target_pairs={{0,128},{16,144},{32,160},{48,176},{64,192},{80,208},{96,224},{112... | collective-permute-start | bytes 2359304 | tf_op jit(solution)/shard_map/ppermute | solution.py:13
  114.7 126.3 %collective-permute-start.8 = (bf16[1024,384]{1,0:T(8,128)(2,1)}, bf16[1024,384]{1,0:T(8,128)(2,1)S(1)}, u32[]{:S(2)}, u32[]{:S(2)}) collective-permute-start(bf16[1024,384]{1,0:T(8,128)(2,1)} %param.15), channel_id=1, source_target_pairs={{0,384},{16,400},{32,416},{48,432},{64,448},{80,464},{96,480},{112... | collective-permute-start | bytes 2359304 | tf_op jit(solution)/shard_map/ppermute | solution.py:13
  120.2 96.1 %copy-start.8 = (bf16[1024,384]{1,0:T(8,128)(2,1)S(1)}, bf16[1024,384]{1,0:T(8,128)(2,1)}, u32[]{:S(2)}) copy-start(bf16[1024,384]{1,0:T(8,128)(2,1)} %param.15) | copy-start | bytes 2359300
  120.2 98.0 %slice-start.1 = ((s8[4718592]{0:T(1024)(128)(4,1)}), s8[4194304]{0:T(1024)(128)(4,1)S(1)}, s32[]{:S(2)}) async-start(s8[4718592]{0:T(1024)(128)(4,1)} %bitcast.32), calls=%async_computation.4 | async-start | bytes 8388608
  216.3 29.2 %collective-permute-start.7 = (bf16[1024,384]{1,0:T(8,128)(2,1)S(1)}, bf16[1024,384]{1,0:T(8,128)(2,1)S(1)}, u32[]{:S(2)}, u32[]{:S(2)}) collective-permute-start(bf16[1024,384]{1,0:T(8,128)(2,1)S(1)} %copy-done.8), channel_id=1, source_target_pairs={{0,256},{16,272},{32,288},{48,304},{64,320},{80,336},{96,352},{112... | collective-permute-start | bytes 2359304 | tf_op jit(solution)/shard_map/ppermute | solution.py:13
  249.2 21.9 %copy-start.6 = (s32[16,2]{0,1:T(2,128)S(1)}, s32[16,2]{0,1:T(2,128)}, u32[]{:S(2)}) copy-start(s32[16,2]{0,1:T(2,128)} %param.10) | copy-start | bytes 388
  250.6 37.4 %all-to-all-start.1 = ((bf16[2,32,12,384]{3,0,2,1:T(2,128)(2,1)}), bf16[2,32,12,384]{3,0,2,1:T(2,128)(2,1)S(1)}, u32[]{:S(2)}, u32[]{:S(2)}) async-start(bf16[2,32,12,384]{3,0,2,1:T(2,128)(2,1)} %copy.28), calls=%async_computation.1 | async-start | bytes 1179648 | tf_op jit(solution)/shard_map/all_to_all | solution.py:81
Sparse Core Ops, SparseCore 0:
  35.2 45.9 all-gather.1
where the time goes:
time: 297 us; the launch traced here: 296 us
  waiting for transfers between devices  132 us (44%)
  blocking collectives  59.5 us (20%)
  starting transfers between devices  56.2 us (19%)
  matrix products  23.7 us (8%)
  between operations  14.5 us (5%)
  other arithmetic  5.73 us (2%)
  local copies, waits for them, and re-layouts  4.15 us (1%)
    ppermute x9, waiting for transfers between devices, passed_along(): lax.ppermute(value, axis, [(i, (i + by) % devices) for i in range(devices)])  92.8 us
    ppermute x9, starting transfers between devices, passed_along(): lax.ppermute(value, axis, [(i, (i + by) % devices) for i in range(devices)])  35.7 us
    all_gather x2, blocking collectives, project(): units = lax.all_gather(hidden, 'exp', axis=1, tiled=True)  34.8 us
    all_to_all x1, blocking collectives, local(): lax.all_to_all(copies, 'tok', split_axis=0, concat_axis=0, tiled=True)  24.7 us
    all_gather x1, waiting for transfers between devices, local(): rows = lax.all_gather(rows_part, 'exp', axis=1, tiled=True)  22.8 us
    all_to_all x1, starting transfers between devices, local(): lax.all_to_all(stacked.astype(jnp.bfloat16), 'tok', split_axis=1, concat_...  20.4 us
    all_to_all x1, waiting for transfers between devices, local(): lax.all_to_all(stacked.astype(jnp.bfloat16), 'tok', split_axis=1, concat_...  16.8 us
    dot_general x2, matrix products, project(): jnp.einsum('sd,fd->sf', rows, gate_w, preferred_element_type=jnp.float32)  11.7 us
  transfers between devices with their start and end apart: 11, of which 4 were waited for; matrix products, arithmetic and copies ran while one was open for 8% of the time, Pallas kernels for 0%

commit v1 on v0

--- a/solution.py
+++ b/solution.py
@@ -2,6 +2,7 @@
 import jax.numpy as jnp
 from jax import lax
 from jax.sharding import PartitionSpec as P
+from jax.lax import all_to_all, axis_size
 
 EXPERTS = 4
 TOP = 2
@@ -44,7 +45,15 @@
         gate = jnp.einsum("sd,fd->sf", rows, gate_w, preferred_element_type=jnp.float32)
         upper = jnp.einsum("sd,fd->sf", rows, up_w, preferred_element_type=jnp.float32)
         hidden = (jax.nn.silu(gate) * upper).astype(jnp.bfloat16)
-        units = lax.all_gather(hidden, "exp", axis=1, tiled=True)
+        units = jnp.concatenate(
+            all_to_all(
+                jnp.stack(tuple((hidden for _ in range(axis_size("exp")))), 0),
+                axis_name="exp",
+                split_axis=0,
+                concat_axis=0,
+            ),
+            1,
+        )
         return jnp.dot(units, down_w, preferred_element_type=jnp.float32)
 
     first = project(w_gate, w_up, w_down)

time: 297 us -> 314 us (1.057)
  starting transfers between devices: 56.2 us -> 99.4 us
  blocking collectives: 59.5 us -> 24.7 us
  local copies, waits for them, and re-layouts: 4.15 us -> 11.8 us
  matrix products: 23.7 us -> 27.1 us
    all_to_all x0 -> x2, starting transfers between devices: none -> 36 us  [project(): all_to_all(jnp.stack(tuple((hidden for _ in range(axis_size('exp')))), 0)...]
    all_gather x2 -> x0, blocking collectives: 34.8 us -> none  [project(): units = lax.all_gather(hidden, 'exp', axis=1, tiled=True)]
    ppermute x9, waiting for transfers between devices: 92.8 us -> 72.2 us  [passed_along(): lax.ppermute(value, axis, [(i, (i + by) % devices) for i in range(devices)])]
    all_gather x1, waiting for transfers between devices: 22.8 us -> 34.6 us  [local(): rows = lax.all_gather(rows_part, 'exp', axis=1, tiled=True)]
    another operation x0 -> x4, local copies, waits for them, and re-layouts: none -> 5.23 us
    all_to_all x0 -> x2, waiting for transfers between devices: none -> 5.12 us  [project(): all_to_all(jnp.stack(tuple((hidden for _ in range(axis_size('exp')))), 0)...]
    all_to_all x1, starting transfers between devices: 20.4 us -> 25.5 us  [local(): lax.all_to_all(stacked.astype(jnp.bfloat16), 'tok', split_axis=1, concat_...]
    dot_general x2, matrix products: 4.13 us -> 7.7 us  [project(): return jnp.dot(units, down_w, preferred_element_type=jnp.float32)]
  transfers between devices with their start and end apart: 11 -> 13, of which waited for: 4 -> 7; matrix products, arithmetic and copies ran while one was open for 8% -> 10% of each run, Pallas kernels for 0% -> 0%
where the time goes in v1:
time: 314 us
  waiting for transfers between devices  131 us (42%)
  starting transfers between devices  99.4 us (32%)
  matrix products  27.1 us (9%)
  blocking collectives  24.7 us (8%)
  between operations  14.4 us (5%)
  local copies, waits for them, and re-layouts  11.8 us (4%)
  other arithmetic  5.6 us (2%)
    ppermute x9, waiting for transfers between devices, passed_along(): lax.ppermute(value, axis, [(i, (i + by) % devices) for i in range(devices)])  72.2 us
    ppermute x9, starting transfers between devices, passed_along(): lax.ppermute(value, axis, [(i, (i + by) % devices) for i in range(devices)])  37.9 us
    all_to_all x2, starting transfers between devices, project(): all_to_all(jnp.stack(tuple((hidden for _ in range(axis_size('exp')))), 0)...  36 us
    all_gather x1, waiting for transfers between devices, local(): rows = lax.all_gather(rows_part, 'exp', axis=1, tiled=True)  34.6 us
    all_to_all x1, starting transfers between devices, local(): lax.all_to_all(stacked.astype(jnp.bfloat16), 'tok', split_axis=1, concat_...  25.5 us
    all_to_all x1, blocking collectives, local(): lax.all_to_all(copies, 'tok', split_axis=0, concat_axis=0, tiled=True)  24.7 us
    all_to_all x1, waiting for transfers between devices, local(): lax.all_to_all(stacked.astype(jnp.bfloat16), 'tok', split_axis=1, concat_...  18.5 us
    dot_general x2, matrix products, project(): jnp.einsum('sd,fd->sf', rows, gate_w, preferred_element_type=jnp.float32)  11.6 us
  transfers between devices with their start and end apart: 13, of which 7 were waited for; matrix products, arithmetic and copies ran while one was open for 10% of the time, Pallas kernels for 0%

profile of v1, /device:TPU:8, one launch (start us, length us, event | category | flops | bytes accessed | tf_op | source)
XLA Modules:
  0.0 313.5 jit_solution(3861222236888419442)
XLA Ops:
  9.6 24.7 %all_to_all.20 = bf16[32,12,384]{2,1,0:T(8,128)(2,1)S(1)} all-to-all(bf16[32,12,384]{2,1,0:T(8,128)(2,1)S(1)} %bitcast.45), channel_id=1, replica_groups=mesh['tok'=32,'exp'=16] {'tok'}, dimensions={0} | all-to-all | bytes 589824 | tf_op jit(solution)/shard_map/all_to_all | solution.py:40
  35.1 3.0 collective-permute-start
  38.1 5.1 %collective-permute-start.2 = (bf16[64,6144]{1,0:T(8,128)(2,1)S(1)}, bf16[64,6144]{1,0:T(8,128)(2,1)}, u32[]{:S(2)}, u32[]{:S(2)}) collective-permute-start(bf16[64,6144]{1,0:T(8,128)(2,1)S(1)} %copy-done.2), channel_id=1, source_target_pairs={{0,384},{16,400},{32,416},{48,432},{64,448},{80,464},{96,480},{112... | collective-permute-start | bytes 2359304 | tf_op jit(solution)/shard_map/ppermute | solution.py:14
  43.2 3.3 %collective-permute-start.1 = (bf16[64,6144]{1,0:T(8,128)(2,1)S(1)}, bf16[64,6144]{1,0:T(8,128)(2,1)}, u32[]{:S(2)}, u32[]{:S(2)}) collective-permute-start(bf16[64,6144]{1,0:T(8,128)(2,1)S(1)} %copy-done.2), channel_id=1, source_target_pairs={{0,256},{16,272},{32,288},{48,304},{64,320},{80,336},{96,352},{112... | collective-permute-start | bytes 2359304 | tf_op jit(solution)/shard_map/ppermute | solution.py:14
  46.5 34.6 %all-gather.2.cloned.1.call-done = bf16[384,6144]{1,0:T(8,128)(2,1)} async-done(((bf16[384,384]{1,0:T(8,128)(2,1)}), bf16[384,6144]{1,0:T(8,128)(2,1)}) %all-gather.2.cloned.1.call-update) | async-done | bytes 4718608 | tf_op jit(solution)/shard_map/all_gather | solution.py:42
  81.1 4.1 %fusion.38 = f32[384,64]{0,1:T(8,128)S(1)} fusion(bf16[384,6144]{1,0:T(8,128)(2,1)} %all-gather.2.cloned.1.call-done, bf16[64,6144]{1,0:T(8,128)(2,1)S(1)} %copy-done.2), kind=kOutput, calls=%fused_computation.64 | convolution fusion | flops 301989888 | bytes 5603328 | tf_op jit(solution)/shard_map/sd,fd->sf/dot_general | solution.py:45
  87.8 4.4 %all-to-all-start.1 = ((bf16[16,384,64]{1,2,0:T(8,128)(2,1)}), bf16[16,384,64]{1,2,0:T(8,128)(2,1)S(1)}, u32[]{:S(2)}, u32[]{:S(2)}) async-start(bf16[16,384,64]{1,2,0:T(8,128)(2,1)} %stack.7), calls=%async_computation.1 | async-start | bytes 1572864 | tf_op jit(solution)/shard_map/all_to_all | solution.py:49
  92.2 4.3 %collective-permute-start.3 = (bf16[64,6144]{1,0:T(8,128)(2,1)S(1)}, bf16[64,6144]{1,0:T(8,128)(2,1)}, u32[]{:S(2)}, u32[]{:S(2)}) collective-permute-start(bf16[64,6144]{1,0:T(8,128)(2,1)S(1)} %copy-done.3), channel_id=1, source_target_pairs={{0,128},{16,144},{32,160},{48,176},{64,192},{80,208},{96,224},{112... | collective-permute-start | bytes 2359304 | tf_op jit(solution)/shard_map/ppermute | solution.py:14
  96.6 3.6 %collective-permute-start.5 = (bf16[64,6144]{1,0:T(8,128)(2,1)S(1)}, bf16[64,6144]{1,0:T(8,128)(2,1)}, u32[]{:S(2)}, u32[]{:S(2)}) collective-permute-start(bf16[64,6144]{1,0:T(8,128)(2,1)S(1)} %copy-done.3), channel_id=1, source_target_pairs={{0,384},{16,400},{32,416},{48,432},{64,448},{80,464},{96,480},{112... | collective-permute-start | bytes 2359304 | tf_op jit(solution)/shard_map/ppermute | solution.py:14
  100.2 6.4 %collective-permute-start.4 = (bf16[64,6144]{1,0:T(8,128)(2,1)S(1)}, bf16[64,6144]{1,0:T(8,128)(2,1)}, u32[]{:S(2)}, u32[]{:S(2)}) collective-permute-start(bf16[64,6144]{1,0:T(8,128)(2,1)S(1)} %copy-done.3), channel_id=1, source_target_pairs={{0,256},{16,272},{32,288},{48,304},{64,320},{80,336},{96,352},{112... | collective-permute-start | bytes 2359304 | tf_op jit(solution)/shard_map/ppermute | solution.py:14
  110.5 3.2 %collective-permute-done.1 = bf16[64,6144]{1,0:T(8,128)(2,1)} collective-permute-done((bf16[64,6144]{1,0:T(8,128)(2,1)S(1)}, bf16[64,6144]{1,0:T(8,128)(2,1)}, u32[]{:S(2)}, u32[]{:S(2)}) %collective-permute-start.1) | collective-permute-done | bytes 786464 | tf_op jit(solution)/shard_map/ppermute | solution.py:14
  113.7 7.5 %fusion.5 = f32[384,64]{0,1:T(8,128)S(1)} fusion(bf16[384,6144]{1,0:T(8,128)(2,1)} %all-gather.2.cloned.1.call-done, bf16[64,6144]{1,0:T(8,128)(2,1)} %collective-permute-done.2, bf16[64,6144]{1,0:T(8,128)(2,1)} %collective-permute-done.1, bf16[64,6144]{1,0:T(8,128)(2,1)} %collective-permute-done, bf16[64,6144]{1,0:T(8,128)(2,1)S(1)} %copy-done.2, ...), kind=kOutput, calls=%fused_computation.14 | convolution fusion | flops 306708480 | bytes 7962640 | tf_op jit(solution)/shard_map/sd,fd->sf/dot_general | solution.py:45
  121.3 38.6 %collective-permute-done.3 = bf16[64,6144]{1,0:T(8,128)(2,1)} collective-permute-done((bf16[64,6144]{1,0:T(8,128)(2,1)S(1)}, bf16[64,6144]{1,0:T(8,128)(2,1)}, u32[]{:S(2)}, u32[]{:S(2)}) %collective-permute-start.3) | collective-permute-done | bytes 786464 | tf_op jit(solution)/shard_map/ppermute | solution.py:14
  159.9 5.9 %multiply_convert_fusion = bf16[384,64]{0,1:T(8,128)(2,1)S(1)} fusion(f32[384,64]{0,1:T(8,128)S(1)} %fusion.5, bf16[384,6144]{1,0:T(8,128)(2,1)S(1)} %bitcast.42, bf16[64,6144]{1,0:T(8,128)(2,1)} %collective-permute-done.5, bf16[64,6144]{1,0:T(8,128)(2,1)} %collective-permute-done.4, bf16[64,6144]{1,0:T(8,128)(2,1)} %collective-permute-done.3, ...), kind=kOutput, calls=%fused_computation.34 | convolution fusion | flops 306855936 | bytes 8011792 | tf_op jit(solution)/shard_map/sd,fd->sf/dot_general | solution.py:46
  166.8 31.6 %all-to-all-start.2 = ((bf16[16,384,64]{1,2,0:T(8,128)(2,1)}), bf16[16,384,64]{1,2,0:T(8,128)(2,1)S(1)}, u32[]{:S(2)}, u32[]{:S(2)}) async-start(bf16[16,384,64]{1,2,0:T(8,128)(2,1)} %stack.8), calls=%async_computation.2 | async-start | bytes 1572864 | tf_op jit(solution)/shard_map/all_to_all | solution.py:49
  198.4 2.3 collective-permute-start.6
  200.6 5.7 %collective-permute-start.8 = (bf16[1024,384]{1,0:T(8,128)(2,1)}, bf16[1024,384]{1,0:T(8,128)(2,1)}, u32[]{:S(2)}, u32[]{:S(2)}) collective-permute-start(bf16[1024,384]{1,0:T(8,128)(2,1)} %param.15), channel_id=1, source_target_pairs={{0,384},{16,400},{32,416},{48,432},{64,448},{80,464},{96,480},{112... | collective-permute-start | bytes 2359304 | tf_op jit(solution)/shard_map/ppermute | solution.py:14
  206.3 4.2 %collective-permute-start.7 = (bf16[1024,384]{1,0:T(8,128)(2,1)}, bf16[1024,384]{1,0:T(8,128)(2,1)}, u32[]{:S(2)}, u32[]{:S(2)}) collective-permute-start(bf16[1024,384]{1,0:T(8,128)(2,1)} %param.15), channel_id=1, source_target_pairs={{0,256},{16,272},{32,288},{48,304},{64,320},{80,336},{96,352},{112... | collective-permute-start | bytes 2359304 | tf_op jit(solution)/shard_map/ppermute | solution.py:14
  213.8 5.1 %all-to-all-done.2 = bf16[16,384,64]{1,2,0:T(8,128)(2,1)S(1)} async-done(((bf16[16,384,64]{1,2,0:T(8,128)(2,1)}), bf16[16,384,64]{1,2,0:T(8,128)(2,1)S(1)}, u32[]{:S(2)}, u32[]{:S(2)}) %all-to-all-start.2) | async-done | bytes 786464 | tf_op jit(solution)/shard_map/all_to_all | solution.py:49
  223.5 26.9 %collective-permute-done.6 = bf16[1024,384]{1,0:T(8,128)(2,1)} collective-permute-done((bf16[1024,384]{1,0:T(8,128)(2,1)}, bf16[1024,384]{1,0:T(8,128)(2,1)}, u32[]{:S(2)}, u32[]{:S(2)}) %collective-permute-start.6) | collective-permute-done | bytes 786464 | tf_op jit(solution)/shard_map/ppermute | solution.py:14
  250.5 3.5 %collective-permute-done.7 = bf16[1024,384]{1,0:T(8,128)(2,1)} collective-permute-done((bf16[1024,384]{1,0:T(8,128)(2,1)}, bf16[1024,384]{1,0:T(8,128)(2,1)}, u32[]{:S(2)}, u32[]{:S(2)}) %collective-permute-start.7) | collective-permute-done | bytes 786464 | tf_op jit(solution)/shard_map/ppermute | solution.py:14
  254.0 5.6 %fusion.1 = bf16[1,32,12,384]{3,1,2,0:T(8,128)(2,1)S(1)} fusion(bf16[1024,384]{1,0:T(8,128)(2,1)} %collective-permute-done.8, bf16[1024,384]{1,0:T(8,128)(2,1)} %collective-permute-done.7, bf16[1024,384]{1,0:T(8,128)(2,1)} %collective-permute-done.6, bf16[1024,384]{1,0:T(8,128)(2,1)} %param.15, bf16[32,12,1024]{2,1,0:T(8,128)(2,1)S(1)} %reshape.107, ...), kind=kOutput, calls=%fused_computation.7 | convolution fusion | flops 306855936 | bytes 4227088 | tf_op jit(solution)/shard_map/dot_general | solution.py:57
  261.1 25.5 %all-to-all-start.3 = ((bf16[2,32,12,384]{3,0,2,1:T(2,128)(2,1)}), bf16[2,32,12,384]{3,0,2,1:T(2,128)(2,1)S(1)}, u32[]{:S(2)}, u32[]{:S(2)}) async-start(bf16[2,32,12,384]{3,0,2,1:T(2,128)(2,1)} %copy.49), calls=%async_computation.3 | async-start | bytes 1179648 | tf_op jit(solution)/shard_map/all_to_all | solution.py:90
  286.7 18.5 %all-to-all-done.3 = bf16[2,32,12,384]{3,0,2,1:T(2,128)(2,1)S(1)} async-done(((bf16[2,32,12,384]{3,0,2,1:T(2,128)(2,1)}), bf16[2,32,12,384]{3,0,2,1:T(2,128)(2,1)S(1)}, u32[]{:S(2)}, u32[]{:S(2)}) %all-to-all-start.3) | async-done | bytes 589856 | tf_op jit(solution)/shard_map/all_to_all | solution.py:90
  (60 shorter events, 21.5 us)
Async XLA Ops:
  7.2 2.2 copy-start
  7.2 27.9 %copy-start.2 = (bf16[64,6144]{1,0:T(8,128)(2,1)S(1)}, bf16[64,6144]{1,0:T(8,128)(2,1)}, u32[]{:S(2)}) copy-start(bf16[64,6144]{1,0:T(8,128)(2,1)} %param.13) | copy-start | bytes 2359300
  7.2 73.9 %all-gather.2.cloned.1.call-start = ((), (), s32[]{:S(2)}) async-start(), calls=%async_computation.4 | async-start | bytes 5013504 | tf_op jit(solution)/shard_map/all_gather | solution.py:42
  35.1 50.1 %copy-start.3 = (bf16[64,6144]{1,0:T(8,128)(2,1)S(1)}, bf16[64,6144]{1,0:T(8,128)(2,1)}, u32[]{:S(2)}) copy-start(bf16[64,6144]{1,0:T(8,128)(2,1)} %param.14) | copy-start | bytes 2359300
  35.1 65.2 %collective-permute-start = (bf16[64,6144]{1,0:T(8,128)(2,1)S(1)}, bf16[64,6144]{1,0:T(8,128)(2,1)}, u32[]{:S(2)}, u32[]{:S(2)}) collective-permute-start(bf16[64,6144]{1,0:T(8,128)(2,1)S(1)} %copy-done.2), channel_id=1, source_target_pairs={{0,128},{16,144},{32,160},{48,176},{64,192},{80,208},{96,224},{112... | collective-permute-start | bytes 2359304 | tf_op jit(solution)/shard_map/ppermute | solution.py:14
  38.1 72.4 %collective-permute-start.2 = (bf16[64,6144]{1,0:T(8,128)(2,1)S(1)}, bf16[64,6144]{1,0:T(8,128)(2,1)}, u32[]{:S(2)}, u32[]{:S(2)}) collective-permute-start(bf16[64,6144]{1,0:T(8,128)(2,1)S(1)} %copy-done.2), channel_id=1, source_target_pairs={{0,384},{16,400},{32,416},{48,432},{64,448},{80,464},{96,480},{112... | collective-permute-start | bytes 2359304 | tf_op jit(solution)/shard_map/ppermute | solution.py:14
  43.2 70.5 %collective-permute-start.1 = (bf16[64,6144]{1,0:T(8,128)(2,1)S(1)}, bf16[64,6144]{1,0:T(8,128)(2,1)}, u32[]{:S(2)}, u32[]{:S(2)}) collective-permute-start(bf16[64,6144]{1,0:T(8,128)(2,1)S(1)} %copy-done.2), channel_id=1, source_target_pairs={{0,256},{16,272},{32,288},{48,304},{64,320},{80,336},{96,352},{112... | collective-permute-start | bytes 2359304 | tf_op jit(solution)/shard_map/ppermute | solution.py:14
  81.1 4.1 %copy-start.1 = (bf16[384,6144]{1,0:T(8,128)(2,1)S(1)}, bf16[384,6144]{1,0:T(8,128)(2,1)}, u32[]{:S(2)}) copy-start(bf16[384,6144]{1,0:T(8,128)(2,1)} %all-gather.2.cloned.1.call-done) | copy-start | bytes 14155780
  86.8 19.9 %copy-start.5 = (s32[4]{0:T(128)S(1)}, s32[4]{0:T(128)}, u32[]{:S(2)}) copy-start(s32[4]{0:T(128)} %param.11) | copy-start | bytes 52
  86.8 20.5 %copy-start.4 = (s32[4]{0:T(128)S(1)}, s32[4]{0:T(128)}, u32[]{:S(2)}) copy-start(s32[4]{0:T(128)} %param.12) | copy-start | bytes 52
  87.8 72.1 %slice-start = ((s8[4718592]{0:T(1024)(128)(4,1)}), s8[524288]{0:T(1024)(128)(4,1)S(1)}, s32[]{:S(2)}) async-start(s8[4718592]{0:T(1024)(128)(4,1)} %bitcast.41), calls=%async_computation.5 | async-start | bytes 1048576
  87.8 78.0 %all-to-all-start.1 = ((bf16[16,384,64]{1,2,0:T(8,128)(2,1)}), bf16[16,384,64]{1,2,0:T(8,128)(2,1)S(1)}, u32[]{:S(2)}, u32[]{:S(2)}) async-start(bf16[16,384,64]{1,2,0:T(8,128)(2,1)} %stack.7), calls=%async_computation.1 | async-start | bytes 1572864 | tf_op jit(solution)/shard_map/all_to_all | solution.py:49
  92.2 67.6 %collective-permute-start.3 = (bf16[64,6144]{1,0:T(8,128)(2,1)S(1)}, bf16[64,6144]{1,0:T(8,128)(2,1)}, u32[]{:S(2)}, u32[]{:S(2)}) collective-permute-start(bf16[64,6144]{1,0:T(8,128)(2,1)S(1)} %copy-done.3), channel_id=1, source_target_pairs={{0,128},{16,144},{32,160},{48,176},{64,192},{80,208},{96,224},{112... | collective-permute-start | bytes 2359304 | tf_op jit(solution)/shard_map/ppermute | solution.py:14
  96.6 63.3 %collective-permute-start.5 = (bf16[64,6144]{1,0:T(8,128)(2,1)S(1)}, bf16[64,6144]{1,0:T(8,128)(2,1)}, u32[]{:S(2)}, u32[]{:S(2)}) collective-permute-start(bf16[64,6144]{1,0:T(8,128)(2,1)S(1)} %copy-done.3), channel_id=1, source_target_pairs={{0,384},{16,400},{32,416},{48,432},{64,448},{80,464},{96,480},{112... | collective-permute-start | bytes 2359304 | tf_op jit(solution)/shard_map/ppermute | solution.py:14
  100.2 59.6 %collective-permute-start.4 = (bf16[64,6144]{1,0:T(8,128)(2,1)S(1)}, bf16[64,6144]{1,0:T(8,128)(2,1)}, u32[]{:S(2)}, u32[]{:S(2)}) collective-permute-start(bf16[64,6144]{1,0:T(8,128)(2,1)S(1)} %copy-done.3), channel_id=1, source_target_pairs={{0,256},{16,272},{32,288},{48,304},{64,320},{80,336},{96,352},{112... | collective-permute-start | bytes 2359304 | tf_op jit(solution)/shard_map/ppermute | solution.py:14
  113.7 46.1 %slice-start.1 = ((s8[4718592]{0:T(1024)(128)(4,1)}), s8[4194304]{0:T(1024)(128)(4,1)S(1)}, s32[]{:S(2)}) async-start(s8[4718592]{0:T(1024)(128)(4,1)} %bitcast.41), calls=%async_computation.6 | async-start | bytes 8388608
  166.8 52.2 %all-to-all-start.2 = ((bf16[16,384,64]{1,2,0:T(8,128)(2,1)}), bf16[16,384,64]{1,2,0:T(8,128)(2,1)S(1)}, u32[]{:S(2)}, u32[]{:S(2)}) async-start(bf16[16,384,64]{1,2,0:T(8,128)(2,1)} %stack.8), calls=%async_computation.2 | async-start | bytes 1572864 | tf_op jit(solution)/shard_map/all_to_all | solution.py:49
  198.4 52.1 %collective-permute-start.6 = (bf16[1024,384]{1,0:T(8,128)(2,1)}, bf16[1024,384]{1,0:T(8,128)(2,1)}, u32[]{:S(2)}, u32[]{:S(2)}) collective-permute-start(bf16[1024,384]{1,0:T(8,128)(2,1)} %param.15), channel_id=1, source_target_pairs={{0,128},{16,144},{32,160},{48,176},{64,192},{80,208},{96,224},{112... | collective-permute-start | bytes 2359304 | tf_op jit(solution)/shard_map/ppermute | solution.py:14
  200.6 49.8 %collective-permute-start.8 = (bf16[1024,384]{1,0:T(8,128)(2,1)}, bf16[1024,384]{1,0:T(8,128)(2,1)}, u32[]{:S(2)}, u32[]{:S(2)}) collective-permute-start(bf16[1024,384]{1,0:T(8,128)(2,1)} %param.15), channel_id=1, source_target_pairs={{0,384},{16,400},{32,416},{48,432},{64,448},{80,464},{96,480},{112... | collective-permute-start | bytes 2359304 | tf_op jit(solution)/shard_map/ppermute | solution.py:14
  206.3 47.6 %collective-permute-start.7 = (bf16[1024,384]{1,0:T(8,128)(2,1)}, bf16[1024,384]{1,0:T(8,128)(2,1)}, u32[]{:S(2)}, u32[]{:S(2)}) collective-permute-start(bf16[1024,384]{1,0:T(8,128)(2,1)} %param.15), channel_id=1, source_target_pairs={{0,256},{16,272},{32,288},{48,304},{64,320},{80,336},{96,352},{112... | collective-permute-start | bytes 2359304 | tf_op jit(solution)/shard_map/ppermute | solution.py:14
  259.6 27.0 %copy-start.6 = (s32[16,2]{0,1:T(2,128)S(1)}, s32[16,2]{0,1:T(2,128)}, u32[]{:S(2)}) copy-start(s32[16,2]{0,1:T(2,128)} %param.10) | copy-start | bytes 388
  261.1 44.1 %all-to-all-start.3 = ((bf16[2,32,12,384]{3,0,2,1:T(2,128)(2,1)}), bf16[2,32,12,384]{3,0,2,1:T(2,128)(2,1)S(1)}, u32[]{:S(2)}, u32[]{:S(2)}) async-start(bf16[2,32,12,384]{3,0,2,1:T(2,128)(2,1)} %copy.49), calls=%async_computation.3 | async-start | bytes 1179648 | tf_op jit(solution)/shard_map/all_to_all | solution.py:90
Sparse Core Ops, SparseCore 0:
  35.2 45.9 all-gather.1
